TPU v7x, 32 devices: a whole 2x2x4 slice. The times are simulated.
32 devices in a mesh: dp: 8 (over z, x), bn: 4 (over y, core).
Axes of the slice: x: 2, y: 2, z: 4, core: 2. Of those that a mesh axis runs over, the one named last changes fastest.
Arguments:
- features: bfloat16 [512, 8, 2048], P(('dp', 'bn')), may hold values from -6 to 6
- shuffle_masks: int32 [16], replicated, may hold values from 0 to 7, as said below
- conv_in: bfloat16 [2048, 512], replicated, may hold values from -0.125 to 0.125
- conv_mid: bfloat16 [3, 512, 512], replicated, may hold values from -0.15625 to 0.15625
- conv_out: bfloat16 [512, 2048], replicated, may hold values from -0.25 to 0.25
- head: bfloat16 [2048, 128], replicated, may hold values from -0.125 to 0.125
- queries: bfloat16 [512, 128], P(('dp', 'bn'))
- queue: bfloat16 [65536, 128], P('dp')
- positive: int32 [512], P(('dp', 'bn')), may hold values from 0 to 511, as said below
Outputs:
- loss_rows: float32 [512], P(('dp', 'bn'))
Inputs may be any that keep to these rules, and one draw needn't show every extreme that they name: `shuffle_masks`: every binary digit of a dp index is set in exactly half of the entries. positive[i] names a crop with the same bn index as crop i.
All inputs are finite; a program needn't handle non-finite values.
Results may differ from a plain program's by a relative error of at most 0.0023.
Values may be sent and summed in bfloat16 or wider, within the bound.
A program may use at most 64 MiB of HBM per device.

v0:
```python
import jax
import jax.numpy as jnp
from jax import lax
from jax.sharding import PartitionSpec as P

EPS_BN = 1e-05
EPS_UNIT = 1e-06
INV_TEMP = 1.0 / 0.07


def partner_2(value, axis, distance):
    return lax.ppermute(value, axis, [(i, i ^ 1 << distance) for i in range(lax.axis_size(axis))])


def unit_rows(values):
    values = values.astype(jnp.float32)
    return values * lax.rsqrt(jnp.sum(values * values, axis=-1, keepdims=True) + EPS_UNIT)


def group_norm(values, row_total):
    first = lax.psum(jnp.sum(values, axis=0), "bn")
    center = first / row_total
    spread = lax.psum(jnp.sum(jnp.square(values - center), axis=0), "bn") / row_total
    return (values - center) * lax.rsqrt(spread + EPS_BN)


def moving_slots(shuffle_masks, level, half):
    flags = jnp.bitwise_and(jnp.right_shift(shuffle_masks, level), 1)
    return jnp.argsort(1 - flags, stable=True)[:half]


def on_device(features, shuffle_masks, conv_in, conv_mid, conv_out, head, queries, queue, positive):
    dp_count = lax.axis_size("dp")
    bn_count = lax.axis_size("bn")
    bit_count = dp_count.bit_length() - 1
    crop_dev, positions, channels = features.shape
    half = crop_dev // 2
    middle = conv_in.shape[1]
    query_unit = unit_rows(queries).astype(jnp.bfloat16)
    query_all = lax.all_gather(query_unit, "dp", axis=0, tiled=True)
    shuffled = features
    for level in range(bit_count):
        moving = moving_slots(shuffle_masks, level, half)
        partner = partner_2(jnp.take(shuffled, moving, axis=0), "dp", level)
        shuffled = shuffled.at[moving].set(partner)
    row_total = crop_dev * positions * bn_count
    flat_rows = shuffled.reshape(crop_dev * positions, channels)
    first_sum = jnp.dot(flat_rows, conv_in, preferred_element_type=jnp.float32)
    first_act = jax.nn.relu(group_norm(first_sum, row_total)).astype(jnp.bfloat16)
    tap_maps = first_act.reshape(crop_dev, positions, middle)
    padded = jnp.pad(tap_maps, ((0, 0), (1, 1), (0, 0)))
    stacked = jnp.concatenate([padded[:, tap : tap + positions, :] for tap in range(3)], axis=2)
    second_sum = jnp.dot(
        stacked.reshape(crop_dev * positions, 3 * middle),
        conv_mid.reshape(3 * middle, middle),
        preferred_element_type=jnp.float32,
    )
    second_act = jax.nn.relu(group_norm(second_sum, row_total)).astype(jnp.bfloat16)
    third_sum = jnp.dot(second_act, conv_out, preferred_element_type=jnp.float32)
    block = jax.nn.relu(group_norm(third_sum, row_total) + flat_rows.astype(jnp.float32)).astype(
        jnp.bfloat16
    )
    pooled = jnp.mean(
        block.reshape(crop_dev, positions, channels).astype(jnp.float32), axis=1
    ).astype(jnp.bfloat16)
    key_unit = unit_rows(jnp.dot(pooled, head, preferred_element_type=jnp.float32)).astype(
        jnp.bfloat16
    )
    for level in range(bit_count):
        moving = moving_slots(shuffle_masks, level, half)
        partner = partner_2(jnp.take(key_unit, moving, axis=0), "dp", level)
        key_unit = key_unit.at[moving].set(partner)
    queue_unit = unit_rows(queue).astype(jnp.bfloat16)
    scores = jnp.dot(query_all, queue_unit.T, preferred_element_type=jnp.float32) * INV_TEMP
    queue_part = jnp.sum(jnp.exp(scores - INV_TEMP), axis=1)
    key_all = lax.all_gather(key_unit, "dp", axis=0, tiled=True)
    slot_of = positive % crop_dev
    column = positive // crop_dev // bn_count
    picked = jnp.take(key_all, column * crop_dev + slot_of, axis=0)
    positive_logit = (
        jnp.sum(query_unit.astype(jnp.float32) * picked.astype(jnp.float32), axis=-1) * INV_TEMP
    )
    negative = lax.psum_scatter(queue_part, "dp", scatter_dimension=0, tiled=True)
    return jnp.log(jnp.exp(positive_logit - INV_TEMP) + negative) + INV_TEMP - positive_logit


def solution(mesh):
    return jax.shard_map(
        on_device,
        mesh=mesh,
        in_specs=(
            P(("dp", "bn"), None, None),
            P(),
            P(),
            P(),
            P(),
            P(),
            P(("dp", "bn"), None),
            P("dp", None),
            P(("dp", "bn")),
        ),
        out_specs=P(("dp", "bn")),
        check_vma=False,
    )
```

profile of v0, /device:TPU:0, one launch (start us, length us, event | category | flops | bytes accessed | tf_op | source)
XLA Modules:
  0.0 185.4 jit_solution(4941348804758811431)
XLA Ops:
  0.0 1.2 copy.17
  1.2 0.7 and_subtract_fusion
  1.9 1.2 sort.51
  3.1 0.6 gather_fusion.1
  3.8 3.0 %collective-permute-start = (bf16[8,8,2048]{2,1,0:T(8,128)(2,1)S(1)}, bf16[8,8,2048]{2,1,0:T(8,128)(2,1)S(1)}, u32[]{:S(2)}, u32[]{:S(2)}) collective-permute-start(bf16[8,8,2048]{2,1,0:T(8,128)(2,1)S(1)} %broadcast_select_fusion.2), channel_id=1, source_target_pairs={{0,4},{4,0},{8,12},{12,8},{16,20},{20,16},{24,28},{28,24},{1,5},{5... | collective-permute-start | bytes 786440 | tf_op jit(solution)/shard_map/ppermute | solution.py:12
  6.8 1.2 sort.52
  8.1 1.2 sort.53
  9.3 3.8 %collective-permute-done = bf16[8,8,2048]{2,1,0:T(8,128)(2,1)S(1)} collective-permute-done((bf16[8,8,2048]{2,1,0:T(8,128)(2,1)S(1)}, bf16[8,8,2048]{2,1,0:T(8,128)(2,1)S(1)}, u32[]{:S(2)}, u32[]{:S(2)}) %collective-permute-start) | collective-permute-done | bytes 262176 | tf_op jit(solution)/shard_map/ppermute | solution.py:12
  13.1 0.8 scatter_fusion
  13.9 0.6 gather_fusion.2
  14.5 1.9 %collective-permute-start.1 = (bf16[8,8,2048]{2,1,0:T(8,128)(2,1)S(1)}, bf16[8,8,2048]{2,1,0:T(8,128)(2,1)S(1)}, u32[]{:S(2)}, u32[]{:S(2)}) collective-permute-start(bf16[8,8,2048]{2,1,0:T(8,128)(2,1)S(1)} %broadcast_select_fusion.1), channel_id=1, source_target_pairs={{0,8},{4,12},{8,0},{12,4},{16,24},{20,28},{24,16},{28,20},{1,9},{5... | collective-permute-start | bytes 786440 | tf_op jit(solution)/shard_map/ppermute | solution.py:12
  16.4 2.7 %fusion.2 = f32[8192]{0:T(1024)S(1)} fusion(bf16[8192,128]{1,0:T(8,128)(2,1)} %param.20), kind=kLoop, calls=%fused_computation.18 | loop fusion | flops 3137536 | bytes 2129920 | tf_op jit(solution)/shard_map/reduce_sum | solution.py:17
  19.2 2.9 %collective-permute-done.1 = bf16[8,8,2048]{2,1,0:T(8,128)(2,1)S(1)} collective-permute-done((bf16[8,8,2048]{2,1,0:T(8,128)(2,1)S(1)}, bf16[8,8,2048]{2,1,0:T(8,128)(2,1)S(1)}, u32[]{:S(2)}, u32[]{:S(2)}) %collective-permute-start.1) | collective-permute-done | bytes 262176 | tf_op jit(solution)/shard_map/ppermute | solution.py:12
  22.1 0.8 scatter_fusion.1
  22.9 0.6 gather_fusion.3
  23.5 2.6 %collective-permute-start.2 = (bf16[8,8,2048]{2,1,0:T(8,128)(2,1)S(1)}, bf16[8,8,2048]{2,1,0:T(8,128)(2,1)S(1)}, u32[]{:S(2)}, u32[]{:S(2)}) collective-permute-start(bf16[8,8,2048]{2,1,0:T(8,128)(2,1)S(1)} %broadcast_select_fusion), channel_id=1, source_target_pairs={{0,16},{4,20},{8,24},{12,28},{16,0},{20,4},{24,8},{28,12},{1,17},{... | collective-permute-start | bytes 786440 | tf_op jit(solution)/shard_map/ppermute | solution.py:12
  26.2 10.5 %collective-permute-done.2 = bf16[8,8,2048]{2,1,0:T(8,128)(2,1)S(1)} collective-permute-done((bf16[8,8,2048]{2,1,0:T(8,128)(2,1)S(1)}, bf16[8,8,2048]{2,1,0:T(8,128)(2,1)S(1)}, u32[]{:S(2)}, u32[]{:S(2)}) %collective-permute-start.2) | collective-permute-done | bytes 262176 | tf_op jit(solution)/shard_map/ppermute | solution.py:12
  36.7 0.8 scatter_fusion.2
  37.4 2.1 %fusion.34 = (f32[512]{0:T(512)S(1)}, f32[128,512]{1,0:T(8,128)S(1)}) fusion(bf16[2048,512]{1,0:T(8,128)(2,1)} %param.15, bf16[16,8,2048]{2,1,0:T(8,128)(2,1)S(1)} %scatter_fusion.2), kind=kOutput, calls=%fused_computation.102 | convolution fusion | flops 268500480 | bytes 2885632 | tf_op jit(solution)/shard_map/dot_general | solution.py:48
  39.5 5.7 %psum.42 = f32[512]{0:T(512)S(1)} all-reduce(f32[512]{0:T(512)S(1)} %get-tuple-element.28), channel_id=1, replica_groups=mesh['dp'=8,'bn'=4] {'bn'}, use_global_device_ids=true, to_apply=%region_8.10 | all-reduce | flops 512 | bytes 4096 | tf_op jit(solution)/shard_map/psum | solution.py:21
  45.2 6.5 %psum.43 = f32[512]{0:T(512)S(1)} all-reduce(f32[512]{0:T(512)S(1)} %multiply_reduce_fusion.2), channel_id=1, replica_groups=mesh['dp'=8,'bn'=4] {'bn'}, use_global_device_ids=true, to_apply=%region_10.12 | all-reduce | flops 512 | bytes 4096 | tf_op jit(solution)/shard_map/psum | solution.py:23
  51.9 1.8 fusion.35
  53.7 5.7 %psum.44 = f32[512]{0:T(512)S(1)} all-reduce(f32[512]{0:T(512)S(1)} %get-tuple-element.30), channel_id=1, replica_groups=mesh['dp'=8,'bn'=4] {'bn'}, use_global_device_ids=true, to_apply=%region_12.14 | all-reduce | flops 512 | bytes 4096 | tf_op jit(solution)/shard_map/psum | solution.py:21
  59.5 6.2 %psum.45 = f32[512]{0:T(512)S(1)} all-reduce(f32[512]{0:T(512)S(1)} %multiply_reduce_fusion.1), channel_id=1, replica_groups=mesh['dp'=8,'bn'=4] {'bn'}, use_global_device_ids=true, to_apply=%region_14.16 | all-reduce | flops 512 | bytes 4096 | tf_op jit(solution)/shard_map/psum | solution.py:23
  65.7 1.4 fusion.36
  67.2 5.9 %psum.46 = f32[2048]{0:T(1024)S(1)} all-reduce(f32[2048]{0:T(1024)S(1)} %get-tuple-element.32), channel_id=1, replica_groups=mesh['dp'=8,'bn'=4] {'bn'}, use_global_device_ids=true, to_apply=%region_16.18 | all-reduce | flops 2048 | bytes 16384 | tf_op jit(solution)/shard_map/psum | solution.py:21
  73.1 1.3 multiply_reduce_fusion
  74.4 6.7 %psum.47 = f32[2048]{0:T(1024)S(1)} all-reduce(f32[2048]{0:T(1024)S(1)} %multiply_reduce_fusion), channel_id=1, replica_groups=mesh['dp'=8,'bn'=4] {'bn'}, use_global_device_ids=true, to_apply=%region_18.20 | all-reduce | flops 2048 | bytes 16384 | tf_op jit(solution)/shard_map/psum | solution.py:23
  81.2 1.7 convert_reduce_fusion
  82.9 0.3 multiply_reduce_fusion.4
  83.3 0.6 gather_fusion.4
  83.9 0.6 collective-permute-start.3
  84.7 2.9 %collective-permute-done.3 = bf16[8,128]{1,0:T(8,128)(2,1)S(1)} collective-permute-done((bf16[8,128]{1,0:T(8,128)(2,1)S(1)}, bf16[8,128]{1,0:T(8,128)(2,1)S(1)}, u32[]{:S(2)}, u32[]{:S(2)}) %collective-permute-start.3) | collective-permute-done | bytes 2080 | tf_op jit(solution)/shard_map/ppermute | solution.py:12
  87.5 0.6 scatter_fusion.3
  88.1 0.6 gather_fusion.5
  89.0 3.3 %collective-permute-done.4 = bf16[8,128]{1,0:T(8,128)(2,1)S(1)} collective-permute-done((bf16[8,128]{1,0:T(8,128)(2,1)S(1)}, bf16[8,128]{1,0:T(8,128)(2,1)S(1)}, u32[]{:S(2)}, u32[]{:S(2)}) %collective-permute-start.4) | collective-permute-done | bytes 2080 | tf_op jit(solution)/shard_map/ppermute | solution.py:12
  92.4 0.6 scatter_fusion.4
  93.0 0.6 gather_fusion.6
  93.6 1.6 collective-permute-start.5
  95.2 0.6 dynamic-slice
  96.5 1.6 collective-permute-done.5
  98.1 0.6 scatter_fusion.5
  98.7 30.4 %all_gather.6 = bf16[128,128]{1,0:T(8,128)(2,1)S(1)} all-gather(bf16[16,128]{1,0:T(8,128)(2,1)S(1)} %scatter_fusion.5), channel_id=1, replica_groups=mesh['dp'=8,'bn'=4] {'dp'}, dimensions={0}, use_global_device_ids=true | all-gather | bytes 36864 | tf_op jit(solution)/shard_map/all_gather | solution.py:76
  129.1 0.6 gather_fusion
  129.9 30.4 %all_gather.7 = bf16[128,128]{1,0:T(8,128)(2,1)S(1)} all-gather(bf16[16,128]{1,0:T(8,128)(2,1)S(1)} %get-tuple-element.14), channel_id=1, replica_groups=mesh['dp'=8,'bn'=4] {'dp'}, dimensions={0}, use_global_device_ids=true | all-gather | bytes 36864 | tf_op jit(solution)/shard_map/all_gather | solution.py:40
  160.3 3.4 %fusion.6 = f32[128]{0:T(128)S(1)} fusion(bf16[128,128]{1,0:T(8,128)(2,1)S(1)} %all_gather.7, bf16[8192,128]{1,0:T(8,128)(2,1)} %param.20, f32[8192]{0:T(1024)S(1)} %add_rsqrt_fusion), kind=kOutput, calls=%fused_computation.21 | convolution fusion | flops 274726784 | bytes 2163200 | tf_op jit(solution)/shard_map/dot_general | solution.py:74
  163.7 21.1 %all-reduce.1 = f32[128]{0:T(128)S(1)} all-reduce(f32[128]{0:T(128)S(1)} %fusion.6), channel_id=2, replica_groups=mesh['dp'=8,'bn'=4] {'dp'}, use_global_device_ids=true, to_apply=%region_27.30.clone | all-reduce | flops 128 | bytes 1024
  184.8 0.6 add_subtract_fusion
  (45 shorter events, 1.5 us)
Async XLA Ops:
  0.0 65.7 %copy-start = (bf16[512,2048]{1,0:T(8,128)(2,1)S(1)}, bf16[512,2048]{1,0:T(8,128)(2,1)}, u32[]{:S(2)}) copy-start(bf16[512,2048]{1,0:T(8,128)(2,1)} %param.17) | copy-start | bytes 6291460
  3.8 9.3 %collective-permute-start = (bf16[8,8,2048]{2,1,0:T(8,128)(2,1)S(1)}, bf16[8,8,2048]{2,1,0:T(8,128)(2,1)S(1)}, u32[]{:S(2)}, u32[]{:S(2)}) collective-permute-start(bf16[8,8,2048]{2,1,0:T(8,128)(2,1)S(1)} %broadcast_select_fusion.2), channel_id=1, source_target_pairs={{0,4},{4,0},{8,12},{12,8},{16,20},{20,16},{24,28},{28,24},{1,5},{5... | collective-permute-start | bytes 786440 | tf_op jit(solution)/shard_map/ppermute | solution.py:12
  14.5 11.6 %copy-start.3 = (s32[16]{0:T(128)S(1)}, s32[16]{0:T(128)}, u32[]{:S(2)}) copy-start(s32[16]{0:T(128)} %param.21) | copy-start | bytes 196
  14.5 7.6 %collective-permute-start.1 = (bf16[8,8,2048]{2,1,0:T(8,128)(2,1)S(1)}, bf16[8,8,2048]{2,1,0:T(8,128)(2,1)S(1)}, u32[]{:S(2)}, u32[]{:S(2)}) collective-permute-start(bf16[8,8,2048]{2,1,0:T(8,128)(2,1)S(1)} %broadcast_select_fusion.1), channel_id=1, source_target_pairs={{0,8},{4,12},{8,0},{12,4},{16,24},{20,28},{24,16},{28,20},{1,9},{5... | collective-permute-start | bytes 786440 | tf_op jit(solution)/shard_map/ppermute | solution.py:12
  23.5 13.2 %collective-permute-start.2 = (bf16[8,8,2048]{2,1,0:T(8,128)(2,1)S(1)}, bf16[8,8,2048]{2,1,0:T(8,128)(2,1)S(1)}, u32[]{:S(2)}, u32[]{:S(2)}) collective-permute-start(bf16[8,8,2048]{2,1,0:T(8,128)(2,1)S(1)} %broadcast_select_fusion), channel_id=1, source_target_pairs={{0,16},{4,20},{8,24},{12,28},{16,0},{20,4},{24,8},{28,12},{1,17},{... | collective-permute-start | bytes 786440 | tf_op jit(solution)/shard_map/ppermute | solution.py:12
  67.2 15.7 %copy-start.1 = (bf16[2048,128]{1,0:T(8,128)(2,1)S(1)}, bf16[2048,128]{1,0:T(8,128)(2,1)}, u32[]{:S(2)}) copy-start(bf16[2048,128]{1,0:T(8,128)(2,1)} %param.18) | copy-start | bytes 1572868
  67.2 17.4 %copy-start.2 = (bf16[16,128]{1,0:T(8,128)(2,1)S(1)}, bf16[16,128]{1,0:T(8,128)(2,1)}, u32[]{:S(2)}) copy-start(bf16[16,128]{1,0:T(8,128)(2,1)} %param.19) | copy-start | bytes 12292
  67.2 28.1 %copy-start.4 = (u32[32]{0:T(128)S(1)}, u32[32]{0:T(128)}, u32[]{:S(2)}) copy-start(u32[32]{0:T(128)} %constant.121) | copy-start | bytes 388
  83.9 3.6 %collective-permute-start.3 = (bf16[8,128]{1,0:T(8,128)(2,1)S(1)}, bf16[8,128]{1,0:T(8,128)(2,1)S(1)}, u32[]{:S(2)}, u32[]{:S(2)}) collective-permute-start(bf16[8,128]{1,0:T(8,128)(2,1)S(1)} %broadcast_select_fusion.5), channel_id=1, source_target_pairs={{0,4},{4,0},{8,12},{12,8},{16,20},{20,16},{24,28},{28,24},{1,5},{5... | collective-permute-start | bytes 6152 | tf_op jit(solution)/shard_map/ppermute | solution.py:12
  88.8 3.6 %collective-permute-start.4 = (bf16[8,128]{1,0:T(8,128)(2,1)S(1)}, bf16[8,128]{1,0:T(8,128)(2,1)S(1)}, u32[]{:S(2)}, u32[]{:S(2)}) collective-permute-start(bf16[8,128]{1,0:T(8,128)(2,1)S(1)} %broadcast_select_fusion.4), channel_id=1, source_target_pairs={{0,8},{4,12},{8,0},{12,4},{16,24},{20,28},{24,16},{28,20},{1,9},{5... | collective-permute-start | bytes 6152 | tf_op jit(solution)/shard_map/ppermute | solution.py:12
  93.6 4.5 %collective-permute-start.5 = (bf16[8,128]{1,0:T(8,128)(2,1)S(1)}, bf16[8,128]{1,0:T(8,128)(2,1)S(1)}, u32[]{:S(2)}, u32[]{:S(2)}) collective-permute-start(bf16[8,128]{1,0:T(8,128)(2,1)S(1)} %broadcast_select_fusion.3), channel_id=1, source_target_pairs={{0,16},{4,20},{8,24},{12,28},{16,0},{20,4},{24,8},{28,12},{1,17},{... | collective-permute-start | bytes 6152 | tf_op jit(solution)/shard_map/ppermute | solution.py:12
where the time goes:
time: 186 us; the launch traced here: 185 us
  blocking collectives  119 us (64%)
  waiting for transfers between devices  25 us (13%)
  other arithmetic  12 us (6%)
  starting transfers between devices  9.94 us (5%)
  local copies, waits for them, and re-layouts  9.89 us (5%)
  matrix products  8.99 us (5%)
    all_gather x1, blocking collectives, on_device(): key_all = lax.all_gather(key_unit, 'dp', axis=0, tiled=True)  30.4 us
    all_gather x1, blocking collectives, on_device(): query_all = lax.all_gather(query_unit, 'dp', axis=0, tiled=True)  30.4 us
    ppermute x6, waiting for transfers between devices, partner_2(): lax.ppermute(value, axis, [(i, i ^ 1 << distance) for i in range(lax.axis...  25 us
    unnamed x1, blocking collectives  21.1 us
    psum x3, blocking collectives, group_norm(): lax.psum(jnp.sum(jnp.square(values - center), axis=0), 'bn') / row_total  19.5 us
    psum x3, blocking collectives, group_norm(): first = lax.psum(jnp.sum(values, axis=0), 'bn')  17.2 us
    ppermute x6, starting transfers between devices, partner_2(): lax.ppermute(value, axis, [(i, i ^ 1 << distance) for i in range(lax.axis...  9.94 us
    sort x3, other arithmetic, moving_slots(): return jnp.argsort(1 - flags, stable=True)[:half]  3.74 us
  transfers between devices with their start and end apart: 6, of which 6 were waited for; matrix products, arithmetic and copies ran while one was open for 3% of the time, Pallas kernels for 0%

commit v1 on v0

--- a/solution.py
+++ b/solution.py
@@ -6,6 +6,23 @@
 EPS_BN = 1e-05
 EPS_UNIT = 1e-06
 INV_TEMP = 1.0 / 0.07
+
+
+def laid_out(blocks, dim):
+    blocks = jnp.moveaxis(blocks, 0, dim)
+    lengths = blocks.shape
+    return blocks.reshape(*lengths[:dim], lengths[dim] * lengths[dim + 1], *lengths[dim + 2 :])
+
+
+def doubled(x, axis):
+    count, place = (lax.axis_size(axis), lax.axis_index(axis))
+    blocks, bit = (x[None], 1)
+    while bit < count:
+        other = lax.ppermute(blocks, axis, [(i, i ^ bit) for i in range(count)])
+        low = place & bit == 0
+        blocks = jnp.concatenate([jnp.where(low, blocks, other), jnp.where(low, other, blocks)])
+        bit *= 2
+    return blocks
 
 
 def partner_2(value, axis, distance):
@@ -73,7 +90,7 @@
     queue_unit = unit_rows(queue).astype(jnp.bfloat16)
     scores = jnp.dot(query_all, queue_unit.T, preferred_element_type=jnp.float32) * INV_TEMP
     queue_part = jnp.sum(jnp.exp(scores - INV_TEMP), axis=1)
-    key_all = lax.all_gather(key_unit, "dp", axis=0, tiled=True)
+    key_all = laid_out(doubled(key_unit, "dp"), 0)
     slot_of = positive % crop_dev
     column = positive // crop_dev // bn_count
     picked = jnp.take(key_all, column * crop_dev + slot_of, axis=0)

time: 186 us -> 168 us (0.903)
  blocking collectives: 119 us -> 88.2 us
  starting transfers between devices: 9.94 us -> 16.3 us
  waiting for transfers between devices: 25 us -> 30.7 us
    all_gather x1 -> x0, blocking collectives: 30.4 us -> none  [on_device(): key_all = lax.all_gather(key_unit, 'dp', axis=0, tiled=True)]
    ppermute x0 -> x3, waiting for transfers between devices: none -> 5.68 us  [doubled(): other = lax.ppermute(blocks, axis, [(i, i ^ bit) for i in range(count)])]
    ppermute x0 -> x3, starting transfers between devices: none -> 5.04 us  [doubled(): other = lax.ppermute(blocks, axis, [(i, i ^ bit) for i in range(count)])]
  transfers between devices with their start and end apart: 6 -> 9, of which waited for: 6 -> 9; matrix products, arithmetic and copies ran while one was open for 3% -> 4% of each run, Pallas kernels for 0% -> 0%
where the time goes in v1:
time: 168 us; the launch traced here: 167 us
  blocking collectives  88.2 us (52%)
  waiting for transfers between devices  30.7 us (18%)
  starting transfers between devices  16.3 us (10%)
  other arithmetic  12 us (7%)
  local copies, waits for them, and re-layouts  9.9 us (6%)
  matrix products  8.97 us (5%)
    all_gather x1, blocking collectives, on_device(): query_all = lax.all_gather(query_unit, 'dp', axis=0, tiled=True)  30.9 us
    ppermute x6, waiting for transfers between devices, partner_2(): lax.ppermute(value, axis, [(i, i ^ 1 << distance) for i in range(lax.axis...  25.1 us
    unnamed x1, blocking collectives  20.6 us
    psum x3, blocking collectives, group_norm(): lax.psum(jnp.sum(jnp.square(values - center), axis=0), 'bn') / row_total  19.5 us
    psum x3, blocking collectives, group_norm(): first = lax.psum(jnp.sum(values, axis=0), 'bn')  17.2 us
    ppermute x6, starting transfers between devices, partner_2(): lax.ppermute(value, axis, [(i, i ^ 1 << distance) for i in range(lax.axis...  11.3 us
    ppermute x3, waiting for transfers between devices, doubled(): other = lax.ppermute(blocks, axis, [(i, i ^ bit) for i in range(count)])  5.68 us
    ppermute x3, starting transfers between devices, doubled(): other = lax.ppermute(blocks, axis, [(i, i ^ bit) for i in range(count)])  5.04 us
  transfers between devices with their start and end apart: 9, of which 9 were waited for; matrix products, arithmetic and copies ran while one was open for 4% of the time, Pallas kernels for 0%

profile of v1, /device:TPU:0, one launch (start us, length us, event | category | flops | bytes accessed | tf_op | source)
XLA Modules:
  0.0 167.1 jit_solution(8252388892318094309)
XLA Ops:
  0.0 1.2 copy.17
  1.2 0.7 and_subtract_fusion
  1.9 1.2 sort.51
  3.8 3.0 %collective-permute-start = (bf16[8,8,2048]{2,1,0:T(8,128)(2,1)S(1)}, bf16[8,8,2048]{2,1,0:T(8,128)(2,1)S(1)}, u32[]{:S(2)}, u32[]{:S(2)}) collective-permute-start(bf16[8,8,2048]{2,1,0:T(8,128)(2,1)S(1)} %broadcast_select_fusion.2), channel_id=1, source_target_pairs={{0,4},{4,0},{8,12},{12,8},{16,20},{20,16},{24,28},{28,24},{1,5},{5... | collective-permute-start | bytes 786440 | tf_op jit(solution)/shard_map/ppermute | solution.py:29
  6.8 1.2 sort.52
  8.0 1.2 sort.53
  9.3 3.8 %collective-permute-done = bf16[8,8,2048]{2,1,0:T(8,128)(2,1)S(1)} collective-permute-done((bf16[8,8,2048]{2,1,0:T(8,128)(2,1)S(1)}, bf16[8,8,2048]{2,1,0:T(8,128)(2,1)S(1)}, u32[]{:S(2)}, u32[]{:S(2)}) %collective-permute-start) | collective-permute-done | bytes 262176 | tf_op jit(solution)/shard_map/ppermute | solution.py:29
  13.1 0.8 scatter_fusion
  14.5 1.9 %collective-permute-start.1 = (bf16[8,8,2048]{2,1,0:T(8,128)(2,1)S(1)}, bf16[8,8,2048]{2,1,0:T(8,128)(2,1)S(1)}, u32[]{:S(2)}, u32[]{:S(2)}) collective-permute-start(bf16[8,8,2048]{2,1,0:T(8,128)(2,1)S(1)} %broadcast_select_fusion.1), channel_id=1, source_target_pairs={{0,8},{4,12},{8,0},{12,4},{16,24},{20,28},{24,16},{28,20},{1,9},{5... | collective-permute-start | bytes 786440 | tf_op jit(solution)/shard_map/ppermute | solution.py:29
  16.4 5.7 %collective-permute-done.1 = bf16[8,8,2048]{2,1,0:T(8,128)(2,1)S(1)} collective-permute-done((bf16[8,8,2048]{2,1,0:T(8,128)(2,1)S(1)}, bf16[8,8,2048]{2,1,0:T(8,128)(2,1)S(1)}, u32[]{:S(2)}, u32[]{:S(2)}) %collective-permute-start.1) | collective-permute-done | bytes 262176 | tf_op jit(solution)/shard_map/ppermute | solution.py:29
  22.1 0.8 scatter_fusion.1
  23.5 2.6 %collective-permute-start.2 = (bf16[8,8,2048]{2,1,0:T(8,128)(2,1)S(1)}, bf16[8,8,2048]{2,1,0:T(8,128)(2,1)S(1)}, u32[]{:S(2)}, u32[]{:S(2)}) collective-permute-start(bf16[8,8,2048]{2,1,0:T(8,128)(2,1)S(1)} %broadcast_select_fusion), channel_id=1, source_target_pairs={{0,16},{4,20},{8,24},{12,28},{16,0},{20,4},{24,8},{28,12},{1,17},{... | collective-permute-start | bytes 786440 | tf_op jit(solution)/shard_map/ppermute | solution.py:29
  26.1 10.6 %collective-permute-done.2 = bf16[8,8,2048]{2,1,0:T(8,128)(2,1)S(1)} collective-permute-done((bf16[8,8,2048]{2,1,0:T(8,128)(2,1)S(1)}, bf16[8,8,2048]{2,1,0:T(8,128)(2,1)S(1)}, u32[]{:S(2)}, u32[]{:S(2)}) %collective-permute-start.2) | collective-permute-done | bytes 262176 | tf_op jit(solution)/shard_map/ppermute | solution.py:29
  36.7 0.8 scatter_fusion.2
  37.4 2.1 %fusion.34 = (f32[512]{0:T(512)S(1)}, f32[128,512]{1,0:T(8,128)S(1)}) fusion(bf16[2048,512]{1,0:T(8,128)(2,1)} %param.15, bf16[16,8,2048]{2,1,0:T(8,128)(2,1)S(1)} %scatter_fusion.2), kind=kOutput, calls=%fused_computation.111 | convolution fusion | flops 268500480 | bytes 2885632 | tf_op jit(solution)/shard_map/dot_general | solution.py:65
  39.5 5.7 %psum.42 = f32[512]{0:T(512)S(1)} all-reduce(f32[512]{0:T(512)S(1)} %get-tuple-element.34), channel_id=1, replica_groups=mesh['dp'=8,'bn'=4] {'bn'}, use_global_device_ids=true, to_apply=%region_8.10 | all-reduce | flops 512 | bytes 4096 | tf_op jit(solution)/shard_map/psum | solution.py:38
  45.2 6.5 %psum.43 = f32[512]{0:T(512)S(1)} all-reduce(f32[512]{0:T(512)S(1)} %multiply_reduce_fusion.2), channel_id=1, replica_groups=mesh['dp'=8,'bn'=4] {'bn'}, use_global_device_ids=true, to_apply=%region_10.12 | all-reduce | flops 512 | bytes 4096 | tf_op jit(solution)/shard_map/psum | solution.py:40
  51.9 1.8 %fusion.35 = (f32[512]{0:T(512)S(1)}, f32[128,512]{1,0:T(8,128)S(1)}) fusion(bf16[1536,512]{1,0:T(8,128)(2,1)} %bitcast.32, bf16[128,512]{1,0:T(8,128)(2,1)S(1)} %get-tuple-element.24, bf16[128,512]{1,0:T(8,128)(2,1)S(1)} %maximum_convert_fusion.2, bf16[128,512]{1,0:T(8,128)(2,1)S(1)} %get-tuple-element.23), kind=kOutput, calls=%fused_computation.112 | convolution fusion | flops 202571264 | bytes 2230272 | tf_op jit(solution)/shard_map/dot_general | solution.py:70
  53.7 5.7 %psum.44 = f32[512]{0:T(512)S(1)} all-reduce(f32[512]{0:T(512)S(1)} %get-tuple-element.36), channel_id=1, replica_groups=mesh['dp'=8,'bn'=4] {'bn'}, use_global_device_ids=true, to_apply=%region_12.14 | all-reduce | flops 512 | bytes 4096 | tf_op jit(solution)/shard_map/psum | solution.py:38
  59.4 6.2 %psum.45 = f32[512]{0:T(512)S(1)} all-reduce(f32[512]{0:T(512)S(1)} %multiply_reduce_fusion.1), channel_id=1, replica_groups=mesh['dp'=8,'bn'=4] {'bn'}, use_global_device_ids=true, to_apply=%region_14.16 | all-reduce | flops 512 | bytes 4096 | tf_op jit(solution)/shard_map/psum | solution.py:40
  65.7 1.4 fusion.36
  67.1 5.9 %psum.46 = f32[2048]{0:T(1024)S(1)} all-reduce(f32[2048]{0:T(1024)S(1)} %get-tuple-element.38), channel_id=1, replica_groups=mesh['dp'=8,'bn'=4] {'bn'}, use_global_device_ids=true, to_apply=%region_16.18 | all-reduce | flops 2048 | bytes 16384 | tf_op jit(solution)/shard_map/psum | solution.py:38
  73.0 1.4 multiply_reduce_fusion
  74.4 6.7 %psum.47 = f32[2048]{0:T(1024)S(1)} all-reduce(f32[2048]{0:T(1024)S(1)} %multiply_reduce_fusion), channel_id=1, replica_groups=mesh['dp'=8,'bn'=4] {'bn'}, use_global_device_ids=true, to_apply=%region_18.20 | all-reduce | flops 2048 | bytes 16384 | tf_op jit(solution)/shard_map/psum | solution.py:40
  81.1 1.7 %convert_reduce_fusion = f32[16,2048]{1,0:T(8,128)S(1)} fusion(bf16[16,8,2048]{2,1,0:T(8,128)(2,1)S(1)} %scatter_fusion.2, f32[2048]{0:T(1024)S(1)} %add_rsqrt_fusion.1, f32[128,2048]{1,0:T(8,128)} %get-tuple-element.39, f32[2048]{0:T(1024)S(1)} %broadcast_multiply_fusion), kind=kLoop, calls=%fused_computation.22 | loop fusion | flops 2064384 | bytes 1720320 | tf_op jit(solution)/shard_map/reduce_sum | solution.py:80
  83.3 0.6 gather_fusion.4
  83.9 0.6 collective-permute-start.3
  84.5 2.7 %fusion.2 = f32[8192]{0:T(1024)S(1)} fusion(bf16[8192,128]{1,0:T(8,128)(2,1)} %param.20), kind=kLoop, calls=%fused_computation.18 | loop fusion | flops 3137536 | bytes 2129920 | tf_op jit(solution)/shard_map/reduce_sum | solution.py:34
  87.5 0.6 scatter_fusion.3
  88.1 0.6 gather_fusion.5
  88.8 0.9 collective-permute-start.4
  89.7 2.7 %collective-permute-done.4 = bf16[8,128]{1,0:T(8,128)(2,1)S(1)} collective-permute-done((bf16[8,128]{1,0:T(8,128)(2,1)S(1)}, bf16[8,128]{1,0:T(8,128)(2,1)S(1)}, u32[]{:S(2)}, u32[]{:S(2)}) %collective-permute-start.4) | collective-permute-done | bytes 2080 | tf_op jit(solution)/shard_map/ppermute | solution.py:29
  92.3 0.6 scatter_fusion.4
  93.6 2.3 %collective-permute-start.5 = (bf16[8,128]{1,0:T(8,128)(2,1)S(1)}, bf16[8,128]{1,0:T(8,128)(2,1)S(1)}, u32[]{:S(2)}, u32[]{:S(2)}) collective-permute-start(bf16[8,128]{1,0:T(8,128)(2,1)S(1)} %broadcast_select_fusion.9), channel_id=1, source_target_pairs={{0,16},{4,20},{8,24},{12,28},{16,0},{20,4},{24,8},{28,12},{1,17},{... | collective-permute-start | bytes 6152 | tf_op jit(solution)/shard_map/ppermute | solution.py:29
  95.9 2.2 %collective-permute-done.5 = bf16[8,128]{1,0:T(8,128)(2,1)S(1)} collective-permute-done((bf16[8,128]{1,0:T(8,128)(2,1)S(1)}, bf16[8,128]{1,0:T(8,128)(2,1)S(1)}, u32[]{:S(2)}, u32[]{:S(2)}) %collective-permute-start.5) | collective-permute-done | bytes 2080 | tf_op jit(solution)/shard_map/ppermute | solution.py:29
  98.1 0.6 scatter_fusion.5
  98.7 1.3 collective-permute-start.6
  100.1 2.3 %collective-permute-done.6 = bf16[1,16,128]{2,1,0:T(8,128)(2,1)S(1)} collective-permute-done((bf16[1,16,128]{2,1,0:T(8,128)(2,1)S(1)}, bf16[1,16,128]{2,1,0:T(8,128)(2,1)S(1)}, u32[]{:S(2)}, u32[]{:S(2)}) %collective-permute-start.6) | collective-permute-done | bytes 4128 | tf_op jit(solution)/shard_map/ppermute | solution.py:21
  102.4 1.4 collective-permute-start.7
  103.8 2.3 %collective-permute-done.7 = bf16[2,16,128]{2,1,0:T(8,128)(2,1)S(1)} collective-permute-done((bf16[2,16,128]{2,1,0:T(8,128)(2,1)S(1)}, bf16[2,16,128]{2,1,0:T(8,128)(2,1)S(1)}, u32[]{:S(2)}, u32[]{:S(2)}) %collective-permute-start.7) | collective-permute-done | bytes 8224 | tf_op jit(solution)/shard_map/ppermute | solution.py:21
  106.1 2.3 %collective-permute-start.8 = (bf16[4,16,128]{2,1,0:T(8,128)(2,1)S(1)}, bf16[4,16,128]{2,1,0:T(8,128)(2,1)S(1)}, u32[]{:S(2)}, u32[]{:S(2)}) collective-permute-start(bf16[4,16,128]{2,1,0:T(8,128)(2,1)S(1)} %pad_maximum_fusion.1), channel_id=1, source_target_pairs={{0,16},{4,20},{8,24},{12,28},{16,0},{20,4},{24,8},{28,12},{1,17},{... | collective-permute-start | bytes 49160 | tf_op jit(solution)/shard_map/ppermute | solution.py:21
  108.5 0.6 dynamic-slice
  109.7 1.1 collective-permute-done.8
  110.8 0.6 gather_fusion
  111.6 30.9 %all_gather.3 = bf16[128,128]{1,0:T(8,128)(2,1)S(1)} all-gather(bf16[16,128]{1,0:T(8,128)(2,1)S(1)} %get-tuple-element.14), channel_id=1, replica_groups=mesh['dp'=8,'bn'=4] {'dp'}, dimensions={0}, use_global_device_ids=true | all-gather | bytes 36864 | tf_op jit(solution)/shard_map/all_gather | solution.py:57
  142.5 3.4 %fusion.6 = f32[128]{0:T(128)S(1)} fusion(bf16[128,128]{1,0:T(8,128)(2,1)S(1)} %all_gather.3, bf16[8192,128]{1,0:T(8,128)(2,1)} %param.20, f32[8192]{0:T(1024)S(1)} %add_rsqrt_fusion), kind=kOutput, calls=%fused_computation.21 | convolution fusion | flops 274726784 | bytes 2163200 | tf_op jit(solution)/shard_map/dot_general | solution.py:91
  145.8 20.6 %all-reduce.1 = f32[128]{0:T(128)S(1)} all-reduce(f32[128]{0:T(128)S(1)} %fusion.6), channel_id=2, replica_groups=mesh['dp'=8,'bn'=4] {'dp'}, use_global_device_ids=true, to_apply=%region_27.30.clone | all-reduce | flops 128 | bytes 1024
  166.5 0.6 add_subtract_fusion
  (56 shorter events, 4.1 us)
Async XLA Ops:
  0.0 65.7 %copy-start = (bf16[512,2048]{1,0:T(8,128)(2,1)S(1)}, bf16[512,2048]{1,0:T(8,128)(2,1)}, u32[]{:S(2)}) copy-start(bf16[512,2048]{1,0:T(8,128)(2,1)} %param.17) | copy-start | bytes 6291460
  3.8 9.3 %collective-permute-start = (bf16[8,8,2048]{2,1,0:T(8,128)(2,1)S(1)}, bf16[8,8,2048]{2,1,0:T(8,128)(2,1)S(1)}, u32[]{:S(2)}, u32[]{:S(2)}) collective-permute-start(bf16[8,8,2048]{2,1,0:T(8,128)(2,1)S(1)} %broadcast_select_fusion.2), channel_id=1, source_target_pairs={{0,4},{4,0},{8,12},{12,8},{16,20},{20,16},{24,28},{28,24},{1,5},{5... | collective-permute-start | bytes 786440 | tf_op jit(solution)/shard_map/ppermute | solution.py:29
  14.5 7.6 %collective-permute-start.1 = (bf16[8,8,2048]{2,1,0:T(8,128)(2,1)S(1)}, bf16[8,8,2048]{2,1,0:T(8,128)(2,1)S(1)}, u32[]{:S(2)}, u32[]{:S(2)}) collective-permute-start(bf16[8,8,2048]{2,1,0:T(8,128)(2,1)S(1)} %broadcast_select_fusion.1), channel_id=1, source_target_pairs={{0,8},{4,12},{8,0},{12,4},{16,24},{20,28},{24,16},{28,20},{1,9},{5... | collective-permute-start | bytes 786440 | tf_op jit(solution)/shard_map/ppermute | solution.py:29
  23.5 13.2 %collective-permute-start.2 = (bf16[8,8,2048]{2,1,0:T(8,128)(2,1)S(1)}, bf16[8,8,2048]{2,1,0:T(8,128)(2,1)S(1)}, u32[]{:S(2)}, u32[]{:S(2)}) collective-permute-start(bf16[8,8,2048]{2,1,0:T(8,128)(2,1)S(1)} %broadcast_select_fusion), channel_id=1, source_target_pairs={{0,16},{4,20},{8,24},{12,28},{16,0},{20,4},{24,8},{28,12},{1,17},{... | collective-permute-start | bytes 786440 | tf_op jit(solution)/shard_map/ppermute | solution.py:29
  67.1 15.7 %copy-start.1 = (bf16[2048,128]{1,0:T(8,128)(2,1)S(1)}, bf16[2048,128]{1,0:T(8,128)(2,1)}, u32[]{:S(2)}) copy-start(bf16[2048,128]{1,0:T(8,128)(2,1)} %param.18) | copy-start | bytes 1572868
  81.1 14.8 %copy-start.3 = (s32[16]{0:T(128)S(1)}, s32[16]{0:T(128)}, u32[]{:S(2)}) copy-start(s32[16]{0:T(128)} %param.21) | copy-start | bytes 196
  81.1 18.8 %copy-start.2 = (bf16[16,128]{1,0:T(8,128)(2,1)S(1)}, bf16[16,128]{1,0:T(8,128)(2,1)}, u32[]{:S(2)}) copy-start(bf16[16,128]{1,0:T(8,128)(2,1)} %param.19) | copy-start | bytes 12292
  81.1 27.3 %copy-start.4 = (u32[32]{0:T(128)S(1)}, u32[32]{0:T(128)}, u32[]{:S(2)}) copy-start(u32[32]{0:T(128)} %constant.129) | copy-start | bytes 388
  83.9 3.6 %collective-permute-start.3 = (bf16[8,128]{1,0:T(8,128)(2,1)S(1)}, bf16[8,128]{1,0:T(8,128)(2,1)S(1)}, u32[]{:S(2)}, u32[]{:S(2)}) collective-permute-start(bf16[8,128]{1,0:T(8,128)(2,1)S(1)} %broadcast_select_fusion.11), channel_id=1, source_target_pairs={{0,4},{4,0},{8,12},{12,8},{16,20},{20,16},{24,28},{28,24},{1,5},{5... | collective-permute-start | bytes 6152 | tf_op jit(solution)/shard_map/ppermute | solution.py:29
  88.8 3.6 %collective-permute-start.4 = (bf16[8,128]{1,0:T(8,128)(2,1)S(1)}, bf16[8,128]{1,0:T(8,128)(2,1)S(1)}, u32[]{:S(2)}, u32[]{:S(2)}) collective-permute-start(bf16[8,128]{1,0:T(8,128)(2,1)S(1)} %broadcast_select_fusion.10), channel_id=1, source_target_pairs={{0,8},{4,12},{8,0},{12,4},{16,24},{20,28},{24,16},{28,20},{1,9},{5... | collective-permute-start | bytes 6152 | tf_op jit(solution)/shard_map/ppermute | solution.py:29
  93.6 4.5 %collective-permute-start.5 = (bf16[8,128]{1,0:T(8,128)(2,1)S(1)}, bf16[8,128]{1,0:T(8,128)(2,1)S(1)}, u32[]{:S(2)}, u32[]{:S(2)}) collective-permute-start(bf16[8,128]{1,0:T(8,128)(2,1)S(1)} %broadcast_select_fusion.9), channel_id=1, source_target_pairs={{0,16},{4,20},{8,24},{12,28},{16,0},{20,4},{24,8},{28,12},{1,17},{... | collective-permute-start | bytes 6152 | tf_op jit(solution)/shard_map/ppermute | solution.py:29
  98.7 3.7 %collective-permute-start.6 = (bf16[1,16,128]{2,1,0:T(8,128)(2,1)S(1)}, bf16[1,16,128]{2,1,0:T(8,128)(2,1)S(1)}, u32[]{:S(2)}, u32[]{:S(2)}) collective-permute-start(bf16[1,16,128]{2,1,0:T(8,128)(2,1)S(1)} %bitcast.30), channel_id=1, source_target_pairs={{0,4},{4,0},{8,12},{12,8},{16,20},{20,16},{24,28},{28,24},{1,5},{5... | collective-permute-start | bytes 12296 | tf_op jit(solution)/shard_map/ppermute | solution.py:21
  102.4 3.7 %collective-permute-start.7 = (bf16[2,16,128]{2,1,0:T(8,128)(2,1)S(1)}, bf16[2,16,128]{2,1,0:T(8,128)(2,1)S(1)}, u32[]{:S(2)}, u32[]{:S(2)}) collective-permute-start(bf16[2,16,128]{2,1,0:T(8,128)(2,1)S(1)} %pad_maximum_fusion.2), channel_id=1, source_target_pairs={{0,8},{4,12},{8,0},{12,4},{16,24},{20,28},{24,16},{28,20},{1,9},{5... | collective-permute-start | bytes 24584 | tf_op jit(solution)/shard_map/ppermute | solution.py:21
  106.1 4.7 %collective-permute-start.8 = (bf16[4,16,128]{2,1,0:T(8,128)(2,1)S(1)}, bf16[4,16,128]{2,1,0:T(8,128)(2,1)S(1)}, u32[]{:S(2)}, u32[]{:S(2)}) collective-permute-start(bf16[4,16,128]{2,1,0:T(8,128)(2,1)S(1)} %pad_maximum_fusion.1), channel_id=1, source_target_pairs={{0,16},{4,20},{8,24},{12,28},{16,0},{20,4},{24,8},{28,12},{1,17},{... | collective-permute-start | bytes 49160 | tf_op jit(solution)/shard_map/ppermute | solution.py:21
